TPU v7x, 512 devices: a whole 4x4x16 slice. The times are simulated.
512 devices in a mesh: dom: 32 (over x_hi, z), grp: 16 (over y, x_lo, core).
Axes of the slice: x: 4 (x_hi: 2, x_lo: 2; x = x_hi * 2 + x_lo), y: 4, z: 16, core: 2. Of those that a mesh axis runs over, the one named last changes fastest.
Arguments:
- adjoint_state: float32 [64, 16, 1024, 256], P('grp', None, 'dom'), may hold values from -6 to 6
- east_wind: float32 [16, 1024, 256], P(None, 'dom'), may hold values from -0.2 to 0.2
- north_wind: float32 [16, 1024, 256], P(None, 'dom'), may hold values from -0.2 to 0.2
- east_diff: float32 [16, 1024, 256], P(None, 'dom'), may hold values from 0.01 to 0.05
- north_diff: float32 [16, 1024, 256], P(None, 'dom'), may hold values from 0.01 to 0.05
- mass_flux: float32 [16, 1024, 256], P(None, 'dom'), may hold values from 0.05 to 0.45
- region_map: int32 [1024, 256], P('dom'), may hold values from 0 to 63
- cloud_top: int32 [1024, 256], P('dom'), may hold values from 1 to 15
Outputs:
- final_adjoint: float32 [64, 16, 1024, 256], P('grp', None, 'dom')
- flux_gradient: float32 [1024, 256], P('dom')
Inputs may be any that keep to these rules, and one draw needn't show every extreme that they name: `region_map`: tag k of the whole set of 64 tags belongs to region k.
All inputs are finite; a program needn't handle non-finite values.
Results may differ from a plain program's by a relative error of at most 0.00002.
Values sent between devices are 32-bit elements; how exact they have to be, the bound alone decides.
A program may use at most 64 MiB of HBM per device.

v0:
```python
import jax
import jax.numpy as jnp
from jax import lax
from jax.sharding import PartitionSpec as P

ITERS = 4


def passed_along(value, axis, by):
    size = lax.axis_size(axis)
    return lax.ppermute(value, axis, [(i, (i + by) % size) for i in range(size)])


def with_halo(cells, sides, width):
    for axis, dim in sides:
        count = lax.axis_size(axis)
        head = lax.slice_in_dim(cells, 0, width, axis=dim)
        tail = lax.slice_in_dim(cells, cells.shape[dim] - width, cells.shape[dim], axis=dim)
        cells = jnp.concatenate(
            [
                lax.ppermute(tail, axis, [(i, (i + 1) % count) for i in range(count)]),
                cells,
                lax.ppermute(head, axis, [((i + 1) % count, i) for i in range(count)]),
            ],
            axis=dim,
        )
    return cells


def local(
    adjoint_state, east_wind, north_wind, east_diff, north_diff, mass_flux, region_map, cloud_top
):
    tags, levels, cols, lats = adjoint_state.shape
    level_ids = lax.broadcasted_iota(jnp.int32, mass_flux.shape, 0)
    active = mass_flux * (level_ids < cloud_top[None]).astype(jnp.float32)
    stacked = jnp.stack([east_wind, east_diff, north_wind, north_diff, active])
    margin = 1
    edge = stacked[0:2, :, cols - 1 : cols]
    left_edge = passed_along(edge, "dom", 1)
    lower_rim = jnp.concatenate(
        [left_edge, jnp.zeros((3,) + left_edge.shape[1:], jnp.float32)], axis=0
    )
    padded = jnp.concatenate([lower_rim, stacked, jnp.zeros_like(lower_rim)], axis=2)
    wind_e = padded[0]
    diff_e = padded[1]
    wind_n = padded[2]
    diff_n = padded[3]
    updraft = padded[4]
    east_coef = jnp.maximum(wind_e, 0.0) + diff_e
    west_prime = jnp.maximum(-wind_e, 0.0) + diff_e
    row_ids = lax.broadcasted_iota(jnp.int32, wind_n.shape, 2)
    north_coef = (jnp.maximum(wind_n, 0.0) + diff_n) * (row_ids < lats - 1).astype(jnp.float32)
    south_prime = jnp.maximum(-wind_n, 0.0) + diff_n
    south_coef = jnp.concatenate(
        [jnp.zeros_like(south_prime[..., :1]), south_prime[..., :-1]], axis=-1
    )
    lam = adjoint_state
    accum = jnp.zeros((tags, cols, lats), jnp.float32)
    for round_step in range(ITERS // margin):
        current = with_halo(lam, (("dom", 2),), 1)
        center = current[:, :, 1 : 1 + cols]
        east = current[:, :, 2 : 2 + cols]
        west = current[:, :, 0:cols]
        coef_e = east_coef[:, margin : margin + cols]
        coef_w = west_prime[:, margin - 1 : margin - 1 + cols]
        coef_n = north_coef[:, margin : margin + cols]
        coef_s = south_coef[:, margin : margin + cols]
        lift = updraft[:, margin : margin + cols]
        north = jnp.concatenate([center[..., 1:], center[..., -1:]], axis=-1)
        south = jnp.concatenate([center[..., :1], center[..., :-1]], axis=-1)
        h = (
            center
            + coef_e * (east - center)
            + coef_w * (west - center)
            + coef_n * (north - center)
            + coef_s * (south - center)
        )
        above = jnp.concatenate([h[:, 1:], h[:, -1:]], axis=1)
        current = h + lift * (above - h)
        accum = accum + current[:, 0, 0:cols]
        lam = current
    tag_ids = lax.axis_index("grp") * tags + lax.broadcasted_iota(jnp.int32, (tags, cols, lats), 0)
    select = (region_map[None] == tag_ids).astype(jnp.float32)
    local_grad = jnp.sum(select * accum, axis=0)
    flux_gradient = lax.psum(local_grad, "grp")
    return (lam, flux_gradient)


def solution(mesh):
    return jax.shard_map(
        local,
        mesh=mesh,
        in_specs=(
            P("grp", None, "dom", None),
            P(None, "dom", None),
            P(None, "dom", None),
            P(None, "dom", None),
            P(None, "dom", None),
            P(None, "dom", None),
            P("dom", None),
            P("dom", None),
        ),
        out_specs=(P("grp", None, "dom", None), P("dom", None)),
        check_vma=False,
    )
```

profile of v0, /device:TPU:4, one launch (start us, length us, event | category | flops | bytes accessed | tf_op | source)
XLA Modules:
  0.0 145.7 jit_solution(17313663855327665156)
XLA Ops:
  1.8 3.8 %collective-permute-start = (f32[2,16,1,256]{3,2,1,0:T(1,128)S(1)}, f32[2,16,1,256]{3,2,1,0:T(1,128)S(1)}, u32[]{:S(2)}, u32[]{:S(2)}) collective-permute-start(f32[2,16,1,256]{3,2,1,0:T(1,128)S(1)} %pad_maximum_fusion.8), channel_id=1, source_target_pairs={{0,16},{16,32},{32,48},{48,64},{64,80},{80,96},{96,112},{112,128},... | collective-permute-start | bytes 98312 | tf_op jit(solution)/shard_map/ppermute | solution.py:11
  6.9 9.4 %collective-permute-start.1 = (f32[4,16,1,256]{3,2,1,0:T(1,128)S(1)}, f32[4,16,1,256]{3,2,1,0:T(1,128)S(1)}, u32[]{:S(2)}, u32[]{:S(2)}) collective-permute-start(f32[4,16,1,256]{3,2,1,0:T(1,128)S(1)} %get-tuple-element.29), channel_id=1, source_target_pairs={{16,0},{32,16},{48,32},{64,48},{80,64},{96,80},{112,96},{128,112},... | collective-permute-start | bytes 196616 | tf_op jit(solution)/shard_map/ppermute | solution.py:23
  16.4 1.9 %collective-permute-start.2 = (f32[4,16,1,256]{3,2,1,0:T(1,128)S(1)}, f32[4,16,1,256]{3,2,1,0:T(1,128)S(1)}, u32[]{:S(2)}, u32[]{:S(2)}) collective-permute-start(f32[4,16,1,256]{3,2,1,0:T(1,128)S(1)} %get-tuple-element.30), channel_id=1, source_target_pairs={{0,16},{16,32},{32,48},{48,64},{64,80},{80,96},{96,112},{112,128},... | collective-permute-start | bytes 196616 | tf_op jit(solution)/shard_map/ppermute | solution.py:21
  18.3 1.9 %constant_dynamic-update-slice_fusion.1 = f32[5,16,32,256]{3,2,1,0:T(8,128)} fusion(f32[16,32,256]{2,1,0:T(8,128)} %param.9), kind=kLoop, calls=%fused_computation.90 | loop fusion | bytes 1048576
  20.2 2.8 %fusion.62 = (f32[4,16,32,255]{3,2,1,0:T(8,128)}, f32[4,16,32,255]{3,2,1,0:T(8,128)}) fusion(f32[4,16,32,256]{3,2,1,0:T(8,128)S(1)} %copy-done), kind=kLoop, calls=%fused_computation.103 | loop fusion | bytes 8355840 | tf_op jit(solution)/shard_map/slice | solution.py:70
  23.0 1.4 fusion.61
  25.2 1.9 %bitcast_dynamic-update-slice_fusion.2 = f32[5,16,32,256]{3,2,1,0:T(8,128)} fusion(f32[5,16,32,256]{3,2,1,0:T(8,128)} %constant_dynamic-update-slice_fusion, f32[16,32,256]{2,1,0:T(8,128)} %param.10), kind=kLoop, calls=%fused_computation.80 | loop fusion | bytes 1048576
  27.1 1.9 %bitcast_dynamic-update-slice_fusion.1 = f32[5,16,32,256]{3,2,1,0:T(8,128)} fusion(f32[5,16,32,256]{3,2,1,0:T(8,128)} %bitcast_dynamic-update-slice_fusion.2, f32[16,32,256]{2,1,0:T(8,128)} %param.12), kind=kLoop, calls=%fused_computation.79 | loop fusion | bytes 1048576
  29.0 1.9 %bitcast_dynamic-update-slice_fusion = f32[5,16,32,256]{3,2,1,0:T(8,128)} fusion(f32[5,16,32,256]{3,2,1,0:T(8,128)} %bitcast_dynamic-update-slice_fusion.1, f32[16,32,256]{2,1,0:T(8,128)} %param.13, s32[32,256]{1,0:T(8,128)S(1)} %copy-done.6), kind=kLoop, calls=%fused_computation.78 | loop fusion | flops 262144 | bytes 1081344 | tf_op jit(solution)/shard_map/stack | solution.py:36
  31.0 2.2 %fusion = f32[5,16,34,256]{3,2,1,0:T(8,128)S(1)} fusion(f32[2,16,1,256]{3,2,1,0:T(1,128)S(1)} %collective-permute-done, f32[5,16,32,256]{3,2,1,0:T(8,128)} %bitcast_dynamic-update-slice_fusion, f32[34]{0:T(128)S(1)} %pad.44.clone), kind=kLoop, calls=%fused_computation.1 | loop fusion | flops 2785280 | bytes 5439624 | tf_op jit(solution)/shard_map/concatenate | solution.py:43
  36.0 1.9 %fusion.29 = f32[4,16,32,256]{3,2,1,0:T(8,128)S(1)} fusion(f32[4,16,32,256]{3,2,1,0:T(8,128)S(1)} %copy-done, f32[4,16,1,256]{3,2,1,0:T(1,128)S(1)} %collective-permute-done.2, f32[4,16,1,256]{3,2,1,0:T(1,128)S(1)} %collective-permute-done.1, f32[4,16,32,1]{3,2,1,0:T(8,128)S(1)} %copy-done.3, f32[4,16,32,255]{3,2,1,0:T(8,128)S(1)} %copy-done.2, ...), kind=kLoop, calls=%fused_computation.38 | loop fusion | flops 8388608 | bytes 10616832 | tf_op jit(solution)/shard_map/add | solution.py:72
  39.9 7.5 %collective-permute-start.3 = (f32[4,16,1,256]{3,2,1,0:T(1,128)S(1)}, f32[4,16,1,256]{3,2,1,0:T(1,128)S(1)}, u32[]{:S(2)}, u32[]{:S(2)}) collective-permute-start(f32[4,16,1,256]{3,2,1,0:T(1,128)S(1)} %get-tuple-element.23), channel_id=1, source_target_pairs={{16,0},{32,16},{48,32},{64,48},{80,64},{96,80},{112,96},{128,112},... | collective-permute-start | bytes 196616 | tf_op jit(solution)/shard_map/ppermute | solution.py:23
  47.4 1.9 %collective-permute-start.4 = (f32[4,16,1,256]{3,2,1,0:T(1,128)S(1)}, f32[4,16,1,256]{3,2,1,0:T(1,128)S(1)}, u32[]{:S(2)}, u32[]{:S(2)}) collective-permute-start(f32[4,16,1,256]{3,2,1,0:T(1,128)S(1)} %get-tuple-element.24), channel_id=1, source_target_pairs={{0,16},{16,32},{32,48},{48,64},{64,80},{80,96},{96,112},{112,128},... | collective-permute-start | bytes 196616 | tf_op jit(solution)/shard_map/ppermute | solution.py:21
  49.7 7.5 %collective-permute-done.4 = f32[4,16,1,256]{3,2,1,0:T(1,128)S(1)} collective-permute-done((f32[4,16,1,256]{3,2,1,0:T(1,128)S(1)}, f32[4,16,1,256]{3,2,1,0:T(1,128)S(1)}, u32[]{:S(2)}, u32[]{:S(2)}) %collective-permute-start.4) | collective-permute-done | bytes 65568 | tf_op jit(solution)/shard_map/ppermute | solution.py:21
  57.2 2.0 %fusion.21 = f32[4,16,32,256]{3,2,1,0:T(8,128)S(1)} fusion(f32[4,16,32,256]{3,2,1,0:T(8,128)S(1)} %fusion.36, f32[4,16,1,256]{3,2,1,0:T(1,128)S(1)} %collective-permute-done.4, f32[4,16,1,256]{3,2,1,0:T(1,128)S(1)} %collective-permute-done.3, f32[4,16,32,1]{3,2,1,0:T(8,128)S(1)} %get-tuple-element.20, f32[4,16,32,255]{3,2,1,0:T(8,128)S(1)} %get-tuple-element.22, ...), kind=kLoop, calls=%fused_computation.28 | loop fusion | flops 8388608 | bytes 10616832 | tf_op jit(solution)/shard_map/add | solution.py:72
  61.1 1.9 %collective-permute-start.5 = (f32[4,16,1,256]{3,2,1,0:T(1,128)S(1)}, f32[4,16,1,256]{3,2,1,0:T(1,128)S(1)}, u32[]{:S(2)}, u32[]{:S(2)}) collective-permute-start(f32[4,16,1,256]{3,2,1,0:T(1,128)S(1)} %get-tuple-element.17), channel_id=1, source_target_pairs={{16,0},{32,16},{48,32},{64,48},{80,64},{96,80},{112,96},{128,112},... | collective-permute-start | bytes 196616 | tf_op jit(solution)/shard_map/ppermute | solution.py:23
  63.1 3.9 %collective-permute-start.6 = (f32[4,16,1,256]{3,2,1,0:T(1,128)S(1)}, f32[4,16,1,256]{3,2,1,0:T(1,128)S(1)}, u32[]{:S(2)}, u32[]{:S(2)}) collective-permute-start(f32[4,16,1,256]{3,2,1,0:T(1,128)S(1)} %get-tuple-element.18), channel_id=1, source_target_pairs={{0,16},{16,32},{32,48},{48,64},{64,80},{80,96},{96,112},{112,128},... | collective-permute-start | bytes 196616 | tf_op jit(solution)/shard_map/ppermute | solution.py:21
  67.4 5.5 %collective-permute-done.6 = f32[4,16,1,256]{3,2,1,0:T(1,128)S(1)} collective-permute-done((f32[4,16,1,256]{3,2,1,0:T(1,128)S(1)}, f32[4,16,1,256]{3,2,1,0:T(1,128)S(1)}, u32[]{:S(2)}, u32[]{:S(2)}) %collective-permute-start.6) | collective-permute-done | bytes 65568 | tf_op jit(solution)/shard_map/ppermute | solution.py:21
  72.8 2.0 %fusion.13 = f32[4,16,32,256]{3,2,1,0:T(8,128)S(1)} fusion(f32[4,16,32,256]{3,2,1,0:T(8,128)S(1)} %fusion.40, f32[4,16,1,256]{3,2,1,0:T(1,128)S(1)} %collective-permute-done.6, f32[4,16,1,256]{3,2,1,0:T(1,128)S(1)} %collective-permute-done.5, f32[4,16,32,1]{3,2,1,0:T(8,128)S(1)} %get-tuple-element.14, f32[4,16,32,255]{3,2,1,0:T(8,128)S(1)} %get-tuple-element.16, ...), kind=kLoop, calls=%fused_computation.18 | loop fusion | flops 8388608 | bytes 10616832 | tf_op jit(solution)/shard_map/add | solution.py:72
  76.6 1.9 %collective-permute-start.7 = (f32[4,16,1,256]{3,2,1,0:T(1,128)S(1)}, f32[4,16,1,256]{3,2,1,0:T(1,128)S(1)}, u32[]{:S(2)}, u32[]{:S(2)}) collective-permute-start(f32[4,16,1,256]{3,2,1,0:T(1,128)S(1)} %get-tuple-element.11), channel_id=1, source_target_pairs={{16,0},{32,16},{48,32},{64,48},{80,64},{96,80},{112,96},{128,112},... | collective-permute-start | bytes 196616 | tf_op jit(solution)/shard_map/ppermute | solution.py:23
  78.6 3.9 %collective-permute-start.8 = (f32[4,16,1,256]{3,2,1,0:T(1,128)S(1)}, f32[4,16,1,256]{3,2,1,0:T(1,128)S(1)}, u32[]{:S(2)}, u32[]{:S(2)}) collective-permute-start(f32[4,16,1,256]{3,2,1,0:T(1,128)S(1)} %get-tuple-element.12), channel_id=1, source_target_pairs={{0,16},{16,32},{32,48},{48,64},{64,80},{80,96},{96,112},{112,128},... | collective-permute-start | bytes 196616 | tf_op jit(solution)/shard_map/ppermute | solution.py:21
  82.9 5.5 %collective-permute-done.8 = f32[4,16,1,256]{3,2,1,0:T(1,128)S(1)} collective-permute-done((f32[4,16,1,256]{3,2,1,0:T(1,128)S(1)}, f32[4,16,1,256]{3,2,1,0:T(1,128)S(1)}, u32[]{:S(2)}, u32[]{:S(2)}) %collective-permute-start.8) | collective-permute-done | bytes 65568 | tf_op jit(solution)/shard_map/ppermute | solution.py:21
  88.3 2.0 %fusion.5 = f32[4,16,32,256]{3,2,1,0:T(8,128)S(1)} fusion(f32[4,16,32,256]{3,2,1,0:T(8,128)S(1)} %fusion.44, f32[4,16,1,256]{3,2,1,0:T(1,128)S(1)} %collective-permute-done.8, f32[4,16,1,256]{3,2,1,0:T(1,128)S(1)} %collective-permute-done.7, f32[4,16,32,1]{3,2,1,0:T(8,128)S(1)} %get-tuple-element.8, f32[4,16,32,255]{3,2,1,0:T(8,128)S(1)} %get-tuple-element.10, ...), kind=kLoop, calls=%fused_computation.8 | loop fusion | flops 8388608 | bytes 10616832 | tf_op jit(solution)/shard_map/add | solution.py:72
  91.5 54.3 %psum.7 = f32[32,256]{1,0:T(8,128)} all-reduce(f32[32,256]{1,0:T(8,128)S(1)} %fusion.51), channel_id=1, replica_groups=mesh['dom'=32,'grp'=16] {'grp'}, use_global_device_ids=true, to_apply=%region_1.0 | all-reduce | flops 8192 | bytes 65536 | tf_op jit(solution)/shard_map/psum | solution.py:85
  (55 shorter events, 13.8 us)
Async XLA Ops:
  0.6 19.6 %copy-start = (f32[4,16,32,256]{3,2,1,0:T(8,128)S(1)}, f32[4,16,32,256]{3,2,1,0:T(8,128)}, u32[]{:S(2)}) copy-start(f32[4,16,32,256]{3,2,1,0:T(8,128)} %param.8) | copy-start | bytes 6291460
  1.8 29.2 %collective-permute-start = (f32[2,16,1,256]{3,2,1,0:T(1,128)S(1)}, f32[2,16,1,256]{3,2,1,0:T(1,128)S(1)}, u32[]{:S(2)}, u32[]{:S(2)}) collective-permute-start(f32[2,16,1,256]{3,2,1,0:T(1,128)S(1)} %pad_maximum_fusion.8), channel_id=1, source_target_pairs={{0,16},{16,32},{32,48},{48,64},{64,80},{80,96},{96,112},{112,128},... | collective-permute-start | bytes 98312 | tf_op jit(solution)/shard_map/ppermute | solution.py:11
  6.9 27.0 %collective-permute-start.1 = (f32[4,16,1,256]{3,2,1,0:T(1,128)S(1)}, f32[4,16,1,256]{3,2,1,0:T(1,128)S(1)}, u32[]{:S(2)}, u32[]{:S(2)}) collective-permute-start(f32[4,16,1,256]{3,2,1,0:T(1,128)S(1)} %get-tuple-element.29), channel_id=1, source_target_pairs={{16,0},{32,16},{48,32},{64,48},{80,64},{96,80},{112,96},{128,112},... | collective-permute-start | bytes 196616 | tf_op jit(solution)/shard_map/ppermute | solution.py:23
  16.4 17.6 %collective-permute-start.2 = (f32[4,16,1,256]{3,2,1,0:T(1,128)S(1)}, f32[4,16,1,256]{3,2,1,0:T(1,128)S(1)}, u32[]{:S(2)}, u32[]{:S(2)}) collective-permute-start(f32[4,16,1,256]{3,2,1,0:T(1,128)S(1)} %get-tuple-element.30), channel_id=1, source_target_pairs={{0,16},{16,32},{32,48},{48,64},{64,80},{80,96},{96,112},{112,128},... | collective-permute-start | bytes 196616 | tf_op jit(solution)/shard_map/ppermute | solution.py:21
  23.0 1.4 copy-start.5
  24.4 4.6 %copy-start.6 = (s32[32,256]{1,0:T(8,128)S(1)}, s32[32,256]{1,0:T(8,128)}, u32[]{:S(2)}) copy-start(s32[32,256]{1,0:T(8,128)} %param.15) | copy-start | bytes 98308
  33.5 1.6 %copy-start.2 = (f32[4,16,32,255]{3,2,1,0:T(8,128)S(1)}, f32[4,16,32,255]{3,2,1,0:T(8,128)}, u32[]{:S(2)}) copy-start(f32[4,16,32,255]{3,2,1,0:T(8,128)} %get-tuple-element.28) | copy-start | bytes 6266884
  33.7 2.1 %copy-start.1 = (f32[4,16,32,255]{3,2,1,0:T(8,128)S(1)}, f32[4,16,32,255]{3,2,1,0:T(8,128)}, u32[]{:S(2)}) copy-start(f32[4,16,32,255]{3,2,1,0:T(8,128)} %get-tuple-element.27) | copy-start | bytes 6266884
  33.7 2.3 %copy-start.3 = (f32[4,16,32,1]{3,2,1,0:T(8,128)S(1)}, f32[4,16,32,1]{3,2,1,0:T(8,128)}, u32[]{:S(2)}) copy-start(f32[4,16,32,1]{3,2,1,0:T(8,128)} %get-tuple-element.26) | copy-start | bytes 24580
  39.9 9.9 %collective-permute-start.3 = (f32[4,16,1,256]{3,2,1,0:T(1,128)S(1)}, f32[4,16,1,256]{3,2,1,0:T(1,128)S(1)}, u32[]{:S(2)}, u32[]{:S(2)}) collective-permute-start(f32[4,16,1,256]{3,2,1,0:T(1,128)S(1)} %get-tuple-element.23), channel_id=1, source_target_pairs={{16,0},{32,16},{48,32},{64,48},{80,64},{96,80},{112,96},{128,112},... | collective-permute-start | bytes 196616 | tf_op jit(solution)/shard_map/ppermute | solution.py:23
  47.4 9.8 %collective-permute-start.4 = (f32[4,16,1,256]{3,2,1,0:T(1,128)S(1)}, f32[4,16,1,256]{3,2,1,0:T(1,128)S(1)}, u32[]{:S(2)}, u32[]{:S(2)}) collective-permute-start(f32[4,16,1,256]{3,2,1,0:T(1,128)S(1)} %get-tuple-element.24), channel_id=1, source_target_pairs={{0,16},{16,32},{32,48},{48,64},{64,80},{80,96},{96,112},{112,128},... | collective-permute-start | bytes 196616 | tf_op jit(solution)/shard_map/ppermute | solution.py:21
  61.1 6.2 %collective-permute-start.5 = (f32[4,16,1,256]{3,2,1,0:T(1,128)S(1)}, f32[4,16,1,256]{3,2,1,0:T(1,128)S(1)}, u32[]{:S(2)}, u32[]{:S(2)}) collective-permute-start(f32[4,16,1,256]{3,2,1,0:T(1,128)S(1)} %get-tuple-element.17), channel_id=1, source_target_pairs={{16,0},{32,16},{48,32},{64,48},{80,64},{96,80},{112,96},{128,112},... | collective-permute-start | bytes 196616 | tf_op jit(solution)/shard_map/ppermute | solution.py:23
  63.1 9.8 %collective-permute-start.6 = (f32[4,16,1,256]{3,2,1,0:T(1,128)S(1)}, f32[4,16,1,256]{3,2,1,0:T(1,128)S(1)}, u32[]{:S(2)}, u32[]{:S(2)}) collective-permute-start(f32[4,16,1,256]{3,2,1,0:T(1,128)S(1)} %get-tuple-element.18), channel_id=1, source_target_pairs={{0,16},{16,32},{32,48},{48,64},{64,80},{80,96},{96,112},{112,128},... | collective-permute-start | bytes 196616 | tf_op jit(solution)/shard_map/ppermute | solution.py:21
  76.6 6.2 %collective-permute-start.7 = (f32[4,16,1,256]{3,2,1,0:T(1,128)S(1)}, f32[4,16,1,256]{3,2,1,0:T(1,128)S(1)}, u32[]{:S(2)}, u32[]{:S(2)}) collective-permute-start(f32[4,16,1,256]{3,2,1,0:T(1,128)S(1)} %get-tuple-element.11), channel_id=1, source_target_pairs={{16,0},{32,16},{48,32},{64,48},{80,64},{96,80},{112,96},{128,112},... | collective-permute-start | bytes 196616 | tf_op jit(solution)/shard_map/ppermute | solution.py:23
  78.6 9.8 %collective-permute-start.8 = (f32[4,16,1,256]{3,2,1,0:T(1,128)S(1)}, f32[4,16,1,256]{3,2,1,0:T(1,128)S(1)}, u32[]{:S(2)}, u32[]{:S(2)}) collective-permute-start(f32[4,16,1,256]{3,2,1,0:T(1,128)S(1)} %get-tuple-element.12), channel_id=1, source_target_pairs={{0,16},{16,32},{32,48},{48,64},{64,80},{80,96},{96,112},{112,128},... | collective-permute-start | bytes 196616 | tf_op jit(solution)/shard_map/ppermute | solution.py:21
  90.6 0.8 copy-start.7
  91.4 54.3 %copy-start.4 = (f32[4,16,32,256]{3,2,1,0:T(8,128)}, f32[4,16,32,256]{3,2,1,0:T(8,128)S(1)}, u32[]{:S(2)}) copy-start(f32[4,16,32,256]{3,2,1,0:T(8,128)S(1)} %fusion.48) | copy-start | bytes 6291460
where the time goes:
time: 146 us
  blocking collectives  54.3 us (37%)
  starting transfers between devices  36.3 us (25%)
  local copies, waits for them, and re-layouts  19.3 us (13%)
  waiting for transfers between devices  18.4 us (13%)
  other arithmetic  16.4 us (11%)
    psum x1, blocking collectives, local(): flux_gradient = lax.psum(local_grad, 'grp')  54.3 us
    ppermute x4, starting transfers between devices, with_halo(): lax.ppermute(head, axis, [((i + 1) % count, i) for i in range(count)])  20.8 us
    ppermute x4, waiting for transfers between devices, with_halo(): lax.ppermute(tail, axis, [(i, (i + 1) % count) for i in range(count)])  18.4 us
    ppermute x4, starting transfers between devices, with_halo(): lax.ppermute(tail, axis, [(i, (i + 1) % count) for i in range(count)])  11.7 us
    unnamed x20, local copies, waits for them, and re-layouts  8.83 us
    add x4, other arithmetic, local(): center + coef_e * (east - center) + coef_w * (west - center)  8 us
    slice x8, local copies, waits for them, and re-layouts, local(): south = jnp.concatenate([center[..., :1], center[..., :-1]], axis=-1)  7.72 us
    ppermute x1, starting transfers between devices, passed_along(): lax.ppermute(value, axis, [(i, (i + by) % size) for i in range(size)])  3.83 us
  transfers between devices with their start and end apart: 9, of which 3 were waited for; matrix products, arithmetic and copies ran while one was open for 12% of the time, Pallas kernels for 0%

commit v1 on v0

--- a/solution.py
+++ b/solution.py
@@ -82,7 +82,7 @@
     tag_ids = lax.axis_index("grp") * tags + lax.broadcasted_iota(jnp.int32, (tags, cols, lats), 0)
     select = (region_map[None] == tag_ids).astype(jnp.float32)
     local_grad = jnp.sum(select * accum, axis=0)
-    flux_gradient = lax.psum(local_grad, "grp")
+    flux_gradient = jnp.sum(lax.all_gather(local_grad, "grp"), axis=0)
     return (lam, flux_gradient)
 
 

time: 146 us -> 118 us (0.81)
  the two profiles are of different devices: /device:TPU:4 before, /device:TPU:1 now
where the time goes in v1:
time: 118 us; the launch traced here: 117 us
  starting transfers between devices  37.7 us (32%)
  blocking collectives  26.1 us (22%)
  local copies, waits for them, and re-layouts  19.3 us (16%)
  other arithmetic  17 us (14%)
  waiting for transfers between devices  16.1 us (14%)
    all_gather x1, blocking collectives, local(): flux_gradient = jnp.sum(lax.all_gather(local_grad, 'grp'), axis=0)  26.1 us
    ppermute x4, starting transfers between devices, with_halo(): lax.ppermute(head, axis, [((i + 1) % count, i) for i in range(count)])  22.8 us
    ppermute x4, waiting for transfers between devices, with_halo(): lax.ppermute(tail, axis, [(i, (i + 1) % count) for i in range(count)])  16 us
    ppermute x4, starting transfers between devices, with_halo(): lax.ppermute(tail, axis, [(i, (i + 1) % count) for i in range(count)])  10.6 us
    unnamed x20, local copies, waits for them, and re-layouts  8.83 us
    add x4, other arithmetic, local(): center + coef_e * (east - center) + coef_w * (west - center)  8 us
    slice x8, local copies, waits for them, and re-layouts, local(): south = jnp.concatenate([center[..., :1], center[..., :-1]], axis=-1)  7.72 us
    ppermute x1, starting transfers between devices, passed_along(): lax.ppermute(value, axis, [(i, (i + by) % size) for i in range(size)])  4.38 us
  transfers between devices with their start and end apart: 9, of which 3 were waited for; matrix products, arithmetic and copies ran while one was open for 15% of the time, Pallas kernels for 0%

profile of v1, /device:TPU:1, one launch (start us, length us, event | category | flops | bytes accessed | tf_op | source)
XLA Modules:
  0.0 117.3 jit_solution(10715594087810283664)
XLA Ops:
  1.8 4.4 %collective-permute-start = (f32[2,16,1,256]{3,2,1,0:T(1,128)S(1)}, f32[2,16,1,256]{3,2,1,0:T(1,128)S(1)}, u32[]{:S(2)}, u32[]{:S(2)}) collective-permute-start(f32[2,16,1,256]{3,2,1,0:T(1,128)S(1)} %pad_maximum_fusion.8), channel_id=1, source_target_pairs={{0,16},{16,32},{32,48},{48,64},{64,80},{80,96},{96,112},{112,128},... | collective-permute-start | bytes 98312 | tf_op jit(solution)/shard_map/ppermute | solution.py:11
  7.5 12.0 %collective-permute-start.1 = (f32[4,16,1,256]{3,2,1,0:T(1,128)S(1)}, f32[4,16,1,256]{3,2,1,0:T(1,128)S(1)}, u32[]{:S(2)}, u32[]{:S(2)}) collective-permute-start(f32[4,16,1,256]{3,2,1,0:T(1,128)S(1)} %get-tuple-element.29), channel_id=1, source_target_pairs={{16,0},{32,16},{48,32},{64,48},{80,64},{96,80},{112,96},{128,112},... | collective-permute-start | bytes 196616 | tf_op jit(solution)/shard_map/ppermute | solution.py:23
  19.4 1.9 %collective-permute-start.2 = (f32[4,16,1,256]{3,2,1,0:T(1,128)S(1)}, f32[4,16,1,256]{3,2,1,0:T(1,128)S(1)}, u32[]{:S(2)}, u32[]{:S(2)}) collective-permute-start(f32[4,16,1,256]{3,2,1,0:T(1,128)S(1)} %get-tuple-element.30), channel_id=1, source_target_pairs={{0,16},{16,32},{32,48},{48,64},{64,80},{80,96},{96,112},{112,128},... | collective-permute-start | bytes 196616 | tf_op jit(solution)/shard_map/ppermute | solution.py:21
  21.4 1.9 %constant_dynamic-update-slice_fusion.1 = f32[5,16,32,256]{3,2,1,0:T(8,128)} fusion(f32[16,32,256]{2,1,0:T(8,128)} %param.9), kind=kLoop, calls=%fused_computation.90 | loop fusion | bytes 1048576
  23.3 2.8 %fusion.62 = (f32[4,16,32,255]{3,2,1,0:T(8,128)}, f32[4,16,32,255]{3,2,1,0:T(8,128)}) fusion(f32[4,16,32,256]{3,2,1,0:T(8,128)S(1)} %copy-done), kind=kLoop, calls=%fused_computation.103 | loop fusion | bytes 8355840 | tf_op jit(solution)/shard_map/slice | solution.py:70
  26.0 1.4 %fusion.61 = (f32[4,16,32,1]{3,2,1,0:T(8,128)S(1)}, f32[4,16,32,1]{3,2,1,0:T(8,128)}) fusion(f32[4,16,32,256]{3,2,1,0:T(8,128)S(1)} %copy-done), kind=kLoop, calls=%fused_computation.102 | loop fusion | bytes 32768 | tf_op jit(solution)/shard_map/slice | solution.py:70
  28.3 1.9 %bitcast_dynamic-update-slice_fusion.2 = f32[5,16,32,256]{3,2,1,0:T(8,128)} fusion(f32[5,16,32,256]{3,2,1,0:T(8,128)} %constant_dynamic-update-slice_fusion, f32[16,32,256]{2,1,0:T(8,128)} %param.10), kind=kLoop, calls=%fused_computation.80 | loop fusion | bytes 1048576
  30.2 1.9 %bitcast_dynamic-update-slice_fusion.1 = f32[5,16,32,256]{3,2,1,0:T(8,128)} fusion(f32[5,16,32,256]{3,2,1,0:T(8,128)} %bitcast_dynamic-update-slice_fusion.2, f32[16,32,256]{2,1,0:T(8,128)} %param.12), kind=kLoop, calls=%fused_computation.79 | loop fusion | bytes 1048576
  32.0 1.9 %bitcast_dynamic-update-slice_fusion = f32[5,16,32,256]{3,2,1,0:T(8,128)} fusion(f32[5,16,32,256]{3,2,1,0:T(8,128)} %bitcast_dynamic-update-slice_fusion.1, f32[16,32,256]{2,1,0:T(8,128)} %param.13, s32[32,256]{1,0:T(8,128)S(1)} %copy-done.6), kind=kLoop, calls=%fused_computation.78 | loop fusion | flops 262144 | bytes 1081344 | tf_op jit(solution)/shard_map/stack | solution.py:36
  34.0 2.2 %fusion = f32[5,16,34,256]{3,2,1,0:T(8,128)S(1)} fusion(f32[2,16,1,256]{3,2,1,0:T(1,128)S(1)} %collective-permute-done, f32[5,16,32,256]{3,2,1,0:T(8,128)} %bitcast_dynamic-update-slice_fusion, f32[34]{0:T(128)S(1)} %pad.44.clone), kind=kLoop, calls=%fused_computation.1 | loop fusion | flops 2785280 | bytes 5439624 | tf_op jit(solution)/shard_map/concatenate | solution.py:43
  39.1 1.9 %fusion.29 = f32[4,16,32,256]{3,2,1,0:T(8,128)S(1)} fusion(f32[4,16,32,256]{3,2,1,0:T(8,128)S(1)} %copy-done, f32[4,16,1,256]{3,2,1,0:T(1,128)S(1)} %collective-permute-done.2, f32[4,16,1,256]{3,2,1,0:T(1,128)S(1)} %collective-permute-done.1, f32[4,16,32,1]{3,2,1,0:T(8,128)S(1)} %copy-done.3, f32[4,16,32,255]{3,2,1,0:T(8,128)S(1)} %copy-done.2, ...), kind=kLoop, calls=%fused_computation.38 | loop fusion | flops 8388608 | bytes 10616832 | tf_op jit(solution)/shard_map/add | solution.py:72
  42.9 7.0 %collective-permute-start.3 = (f32[4,16,1,256]{3,2,1,0:T(1,128)S(1)}, f32[4,16,1,256]{3,2,1,0:T(1,128)S(1)}, u32[]{:S(2)}, u32[]{:S(2)}) collective-permute-start(f32[4,16,1,256]{3,2,1,0:T(1,128)S(1)} %get-tuple-element.23), channel_id=1, source_target_pairs={{16,0},{32,16},{48,32},{64,48},{80,64},{96,80},{112,96},{128,112},... | collective-permute-start | bytes 196616 | tf_op jit(solution)/shard_map/ppermute | solution.py:23
  49.9 1.9 %collective-permute-start.4 = (f32[4,16,1,256]{3,2,1,0:T(1,128)S(1)}, f32[4,16,1,256]{3,2,1,0:T(1,128)S(1)}, u32[]{:S(2)}, u32[]{:S(2)}) collective-permute-start(f32[4,16,1,256]{3,2,1,0:T(1,128)S(1)} %get-tuple-element.24), channel_id=1, source_target_pairs={{0,16},{16,32},{32,48},{48,64},{64,80},{80,96},{96,112},{112,128},... | collective-permute-start | bytes 196616 | tf_op jit(solution)/shard_map/ppermute | solution.py:21
  52.2 6.3 %collective-permute-done.4 = f32[4,16,1,256]{3,2,1,0:T(1,128)S(1)} collective-permute-done((f32[4,16,1,256]{3,2,1,0:T(1,128)S(1)}, f32[4,16,1,256]{3,2,1,0:T(1,128)S(1)}, u32[]{:S(2)}, u32[]{:S(2)}) %collective-permute-start.4) | collective-permute-done | bytes 65568 | tf_op jit(solution)/shard_map/ppermute | solution.py:21
  58.5 2.0 %fusion.21 = f32[4,16,32,256]{3,2,1,0:T(8,128)S(1)} fusion(f32[4,16,32,256]{3,2,1,0:T(8,128)S(1)} %fusion.36, f32[4,16,1,256]{3,2,1,0:T(1,128)S(1)} %collective-permute-done.4, f32[4,16,1,256]{3,2,1,0:T(1,128)S(1)} %collective-permute-done.3, f32[4,16,32,1]{3,2,1,0:T(8,128)S(1)} %get-tuple-element.20, f32[4,16,32,255]{3,2,1,0:T(8,128)S(1)} %get-tuple-element.22, ...), kind=kLoop, calls=%fused_computation.28 | loop fusion | flops 8388608 | bytes 10616832 | tf_op jit(solution)/shard_map/add | solution.py:72
  62.5 1.9 %collective-permute-start.5 = (f32[4,16,1,256]{3,2,1,0:T(1,128)S(1)}, f32[4,16,1,256]{3,2,1,0:T(1,128)S(1)}, u32[]{:S(2)}, u32[]{:S(2)}) collective-permute-start(f32[4,16,1,256]{3,2,1,0:T(1,128)S(1)} %get-tuple-element.17), channel_id=1, source_target_pairs={{16,0},{32,16},{48,32},{64,48},{80,64},{96,80},{112,96},{128,112},... | collective-permute-start | bytes 196616 | tf_op jit(solution)/shard_map/ppermute | solution.py:23
  64.4 3.4 %collective-permute-start.6 = (f32[4,16,1,256]{3,2,1,0:T(1,128)S(1)}, f32[4,16,1,256]{3,2,1,0:T(1,128)S(1)}, u32[]{:S(2)}, u32[]{:S(2)}) collective-permute-start(f32[4,16,1,256]{3,2,1,0:T(1,128)S(1)} %get-tuple-element.18), channel_id=1, source_target_pairs={{0,16},{16,32},{32,48},{48,64},{64,80},{80,96},{96,112},{112,128},... | collective-permute-start | bytes 196616 | tf_op jit(solution)/shard_map/ppermute | solution.py:21
  68.2 4.9 %collective-permute-done.6 = f32[4,16,1,256]{3,2,1,0:T(1,128)S(1)} collective-permute-done((f32[4,16,1,256]{3,2,1,0:T(1,128)S(1)}, f32[4,16,1,256]{3,2,1,0:T(1,128)S(1)}, u32[]{:S(2)}, u32[]{:S(2)}) %collective-permute-start.6) | collective-permute-done | bytes 65568 | tf_op jit(solution)/shard_map/ppermute | solution.py:21
  73.0 2.0 %fusion.13 = f32[4,16,32,256]{3,2,1,0:T(8,128)S(1)} fusion(f32[4,16,32,256]{3,2,1,0:T(8,128)S(1)} %fusion.40, f32[4,16,1,256]{3,2,1,0:T(1,128)S(1)} %collective-permute-done.6, f32[4,16,1,256]{3,2,1,0:T(1,128)S(1)} %collective-permute-done.5, f32[4,16,32,1]{3,2,1,0:T(8,128)S(1)} %get-tuple-element.14, f32[4,16,32,255]{3,2,1,0:T(8,128)S(1)} %get-tuple-element.16, ...), kind=kLoop, calls=%fused_computation.18 | loop fusion | flops 8388608 | bytes 10616832 | tf_op jit(solution)/shard_map/add | solution.py:72
  76.8 1.9 %collective-permute-start.7 = (f32[4,16,1,256]{3,2,1,0:T(1,128)S(1)}, f32[4,16,1,256]{3,2,1,0:T(1,128)S(1)}, u32[]{:S(2)}, u32[]{:S(2)}) collective-permute-start(f32[4,16,1,256]{3,2,1,0:T(1,128)S(1)} %get-tuple-element.11), channel_id=1, source_target_pairs={{16,0},{32,16},{48,32},{64,48},{80,64},{96,80},{112,96},{128,112},... | collective-permute-start | bytes 196616 | tf_op jit(solution)/shard_map/ppermute | solution.py:23
  78.8 3.4 %collective-permute-start.8 = (f32[4,16,1,256]{3,2,1,0:T(1,128)S(1)}, f32[4,16,1,256]{3,2,1,0:T(1,128)S(1)}, u32[]{:S(2)}, u32[]{:S(2)}) collective-permute-start(f32[4,16,1,256]{3,2,1,0:T(1,128)S(1)} %get-tuple-element.12), channel_id=1, source_target_pairs={{0,16},{16,32},{32,48},{48,64},{64,80},{80,96},{96,112},{112,128},... | collective-permute-start | bytes 196616 | tf_op jit(solution)/shard_map/ppermute | solution.py:21
  82.5 4.9 %collective-permute-done.8 = f32[4,16,1,256]{3,2,1,0:T(1,128)S(1)} collective-permute-done((f32[4,16,1,256]{3,2,1,0:T(1,128)S(1)}, f32[4,16,1,256]{3,2,1,0:T(1,128)S(1)}, u32[]{:S(2)}, u32[]{:S(2)}) %collective-permute-start.8) | collective-permute-done | bytes 65568 | tf_op jit(solution)/shard_map/ppermute | solution.py:21
  87.4 2.0 %fusion.5 = f32[4,16,32,256]{3,2,1,0:T(8,128)S(1)} fusion(f32[4,16,32,256]{3,2,1,0:T(8,128)S(1)} %fusion.44, f32[4,16,1,256]{3,2,1,0:T(1,128)S(1)} %collective-permute-done.8, f32[4,16,1,256]{3,2,1,0:T(1,128)S(1)} %collective-permute-done.7, f32[4,16,32,1]{3,2,1,0:T(8,128)S(1)} %get-tuple-element.8, f32[4,16,32,255]{3,2,1,0:T(8,128)S(1)} %get-tuple-element.10, ...), kind=kLoop, calls=%fused_computation.8 | loop fusion | flops 8388608 | bytes 10616832 | tf_op jit(solution)/shard_map/add | solution.py:72
  90.5 26.1 %all-gather = f32[512,256]{1,0:T(8,128)S(1)} all-gather(f32[32,256]{1,0:T(8,128)S(1)} %fusion.51), channel_id=2, replica_groups=mesh['dom'=32,'grp'=16] {'grp'}, dimensions={0}, use_global_device_ids=true | all-gather | bytes 557056 | tf_op jit(solution)/shard_map/all_gather | solution.py:85
  (56 shorter events, 14.5 us)
Async XLA Ops:
  0.6 22.6 %copy-start = (f32[4,16,32,256]{3,2,1,0:T(8,128)S(1)}, f32[4,16,32,256]{3,2,1,0:T(8,128)}, u32[]{:S(2)}) copy-start(f32[4,16,32,256]{3,2,1,0:T(8,128)} %param.8) | copy-start | bytes 6291460
  1.8 32.2 %collective-permute-start = (f32[2,16,1,256]{3,2,1,0:T(1,128)S(1)}, f32[2,16,1,256]{3,2,1,0:T(1,128)S(1)}, u32[]{:S(2)}, u32[]{:S(2)}) collective-permute-start(f32[2,16,1,256]{3,2,1,0:T(1,128)S(1)} %pad_maximum_fusion.8), channel_id=1, source_target_pairs={{0,16},{16,32},{32,48},{48,64},{64,80},{80,96},{96,112},{112,128},... | collective-permute-start | bytes 98312 | tf_op jit(solution)/shard_map/ppermute | solution.py:11
  7.5 29.5 %collective-permute-start.1 = (f32[4,16,1,256]{3,2,1,0:T(1,128)S(1)}, f32[4,16,1,256]{3,2,1,0:T(1,128)S(1)}, u32[]{:S(2)}, u32[]{:S(2)}) collective-permute-start(f32[4,16,1,256]{3,2,1,0:T(1,128)S(1)} %get-tuple-element.29), channel_id=1, source_target_pairs={{16,0},{32,16},{48,32},{64,48},{80,64},{96,80},{112,96},{128,112},... | collective-permute-start | bytes 196616 | tf_op jit(solution)/shard_map/ppermute | solution.py:23
  19.4 17.6 %collective-permute-start.2 = (f32[4,16,1,256]{3,2,1,0:T(1,128)S(1)}, f32[4,16,1,256]{3,2,1,0:T(1,128)S(1)}, u32[]{:S(2)}, u32[]{:S(2)}) collective-permute-start(f32[4,16,1,256]{3,2,1,0:T(1,128)S(1)} %get-tuple-element.30), channel_id=1, source_target_pairs={{0,16},{16,32},{32,48},{48,64},{64,80},{80,96},{96,112},{112,128},... | collective-permute-start | bytes 196616 | tf_op jit(solution)/shard_map/ppermute | solution.py:21
  26.0 1.4 %copy-start.5 = (f32[16,32,256]{2,1,0:T(8,128)S(1)}, f32[16,32,256]{2,1,0:T(8,128)}, u32[]{:S(2)}) copy-start(f32[16,32,256]{2,1,0:T(8,128)} %param.11) | copy-start | bytes 1572868
  27.4 4.6 %copy-start.6 = (s32[32,256]{1,0:T(8,128)S(1)}, s32[32,256]{1,0:T(8,128)}, u32[]{:S(2)}) copy-start(s32[32,256]{1,0:T(8,128)} %param.15) | copy-start | bytes 98308
  36.6 1.6 %copy-start.2 = (f32[4,16,32,255]{3,2,1,0:T(8,128)S(1)}, f32[4,16,32,255]{3,2,1,0:T(8,128)}, u32[]{:S(2)}) copy-start(f32[4,16,32,255]{3,2,1,0:T(8,128)} %get-tuple-element.28) | copy-start | bytes 6266884
  36.8 2.1 %copy-start.1 = (f32[4,16,32,255]{3,2,1,0:T(8,128)S(1)}, f32[4,16,32,255]{3,2,1,0:T(8,128)}, u32[]{:S(2)}) copy-start(f32[4,16,32,255]{3,2,1,0:T(8,128)} %get-tuple-element.27) | copy-start | bytes 6266884
  36.8 2.3 %copy-start.3 = (f32[4,16,32,1]{3,2,1,0:T(8,128)S(1)}, f32[4,16,32,1]{3,2,1,0:T(8,128)}, u32[]{:S(2)}) copy-start(f32[4,16,32,1]{3,2,1,0:T(8,128)} %get-tuple-element.26) | copy-start | bytes 24580
  42.9 9.3 %collective-permute-start.3 = (f32[4,16,1,256]{3,2,1,0:T(1,128)S(1)}, f32[4,16,1,256]{3,2,1,0:T(1,128)S(1)}, u32[]{:S(2)}, u32[]{:S(2)}) collective-permute-start(f32[4,16,1,256]{3,2,1,0:T(1,128)S(1)} %get-tuple-element.23), channel_id=1, source_target_pairs={{16,0},{32,16},{48,32},{64,48},{80,64},{96,80},{112,96},{128,112},... | collective-permute-start | bytes 196616 | tf_op jit(solution)/shard_map/ppermute | solution.py:23
  49.9 8.6 %collective-permute-start.4 = (f32[4,16,1,256]{3,2,1,0:T(1,128)S(1)}, f32[4,16,1,256]{3,2,1,0:T(1,128)S(1)}, u32[]{:S(2)}, u32[]{:S(2)}) collective-permute-start(f32[4,16,1,256]{3,2,1,0:T(1,128)S(1)} %get-tuple-element.24), channel_id=1, source_target_pairs={{0,16},{16,32},{32,48},{48,64},{64,80},{80,96},{96,112},{112,128},... | collective-permute-start | bytes 196616 | tf_op jit(solution)/shard_map/ppermute | solution.py:21
  62.5 5.7 %collective-permute-start.5 = (f32[4,16,1,256]{3,2,1,0:T(1,128)S(1)}, f32[4,16,1,256]{3,2,1,0:T(1,128)S(1)}, u32[]{:S(2)}, u32[]{:S(2)}) collective-permute-start(f32[4,16,1,256]{3,2,1,0:T(1,128)S(1)} %get-tuple-element.17), channel_id=1, source_target_pairs={{16,0},{32,16},{48,32},{64,48},{80,64},{96,80},{112,96},{128,112},... | collective-permute-start | bytes 196616 | tf_op jit(solution)/shard_map/ppermute | solution.py:23
  64.4 8.6 %collective-permute-start.6 = (f32[4,16,1,256]{3,2,1,0:T(1,128)S(1)}, f32[4,16,1,256]{3,2,1,0:T(1,128)S(1)}, u32[]{:S(2)}, u32[]{:S(2)}) collective-permute-start(f32[4,16,1,256]{3,2,1,0:T(1,128)S(1)} %get-tuple-element.18), channel_id=1, source_target_pairs={{0,16},{16,32},{32,48},{48,64},{64,80},{80,96},{96,112},{112,128},... | collective-permute-start | bytes 196616 | tf_op jit(solution)/shard_map/ppermute | solution.py:21
  76.8 5.7 %collective-permute-start.7 = (f32[4,16,1,256]{3,2,1,0:T(1,128)S(1)}, f32[4,16,1,256]{3,2,1,0:T(1,128)S(1)}, u32[]{:S(2)}, u32[]{:S(2)}) collective-permute-start(f32[4,16,1,256]{3,2,1,0:T(1,128)S(1)} %get-tuple-element.11), channel_id=1, source_target_pairs={{16,0},{32,16},{48,32},{64,48},{80,64},{96,80},{112,96},{128,112},... | collective-permute-start | bytes 196616 | tf_op jit(solution)/shard_map/ppermute | solution.py:23
  78.8 8.6 %collective-permute-start.8 = (f32[4,16,1,256]{3,2,1,0:T(1,128)S(1)}, f32[4,16,1,256]{3,2,1,0:T(1,128)S(1)}, u32[]{:S(2)}, u32[]{:S(2)}) collective-permute-start(f32[4,16,1,256]{3,2,1,0:T(1,128)S(1)} %get-tuple-element.12), channel_id=1, source_target_pairs={{0,16},{16,32},{32,48},{48,64},{64,80},{80,96},{96,112},{112,128},... | collective-permute-start | bytes 196616 | tf_op jit(solution)/shard_map/ppermute | solution.py:21
  89.7 0.8 copy-start.7
  90.4 26.8 %copy-start.4 = (f32[4,16,32,256]{3,2,1,0:T(8,128)}, f32[4,16,32,256]{3,2,1,0:T(8,128)S(1)}, u32[]{:S(2)}) copy-start(f32[4,16,32,256]{3,2,1,0:T(8,128)S(1)} %fusion.48) | copy-start | bytes 6291460
